TPU v7x, 32 devices: a whole 2x2x4 slice. The times are simulated.
32 devices in a mesh: dp: 2 (over x), row: 4 (over z), col: 4 (over y, core).
Axes of the slice: x: 2, y: 2, z: 4, core: 2. Of those that a mesh axis runs over, the one named last changes fastest.
Arguments:
- tokens: bfloat16 [16, 768, 1024], P(('dp', 'row'), 'col'), may hold values from -6 to 6
- memory: bfloat16 [16, 20, 768], P(('dp', 'row'), None, 'col'), may hold values from -6 to 6
- block_ids: int32 [16, 1024], P(('dp', 'row')), may hold values from 0 to 7, never falling along the last dimension, each value on 1 to 256 neighbouring positions
- valid: int32 [16], replicated, may hold values from 512 to 1024
- teacher: bfloat16 [16, 768, 1024], P(('dp', 'row'), 'col'), may hold values from -6 to 6
- w_qkv: bfloat16 [12, 147456], P('row', 'col'), may hold values from -0.21875 to 0.21875
- bias_qv: float32 [12, 128], P('row'), may hold values from -3 to 3
- w_out: bfloat16 [768, 768], P('row', 'col'), may hold values from -0.875 to 0.875
- bias_out: float32 [768], P('col'), may hold values from -2 to 2
- ln1_gain: float32 [768], P('col'), may hold values from 0.1 to 1.9
- ln1_bias: float32 [768], P('col'), may hold values from -2 to 2
- w_up: bfloat16 [768, 3072], P('col', 'row'), may hold values from -0.21875 to 0.21875
- bias_up: float32 [3072], P('row'), may hold values from -3 to 3
- w_down: bfloat16 [768, 3072], P('col', 'row'), may hold values from -0.109375 to 0.109375
- bias_down: float32 [768], P('col'), may hold values from -2 to 2
- ln2_gain: float32 [768], P('col'), may hold values from 0.1 to 1.9
- ln2_bias: float32 [768], P('col'), may hold values from -2 to 2
Outputs:
- layer_out: bfloat16 [16, 1044, 768], P(('dp', 'row'), None, 'col')
- grad_tokens: float32 [16, 1024, 768], P(('dp', 'row'), None, 'col')
- grad_memory: float32 [16, 20, 768], P(('dp', 'row'), None, 'col')
- grad_w_qkv: float32 [12, 147456], P('row', 'col')
- grad_bias_qv: float32 [12, 128], P('row')
- grad_w_out: float32 [768, 768], P('row', 'col')
- grad_bias_out: float32 [768], P('col')
- grad_ln1_gain: float32 [768], P('col')
- grad_ln1_bias: float32 [768], P('col')
- grad_w_up: float32 [768, 3072], P('col', 'row')
- grad_bias_up: float32 [3072], P('row')
- grad_w_down: float32 [768, 3072], P('col', 'row')
- grad_bias_down: float32 [768], P('col')
- grad_ln2_gain: float32 [768], P('col')
- grad_ln2_bias: float32 [768], P('col')
Inputs may be any that keep to these rules, and one draw needn't show every extreme that they name: `block_ids`: along each sequence the numbers never fall; each of the 8 numbers covers 1 to 256 consecutive tokens.
All inputs are finite; a program needn't handle non-finite values.
Results may differ from a plain program's by a relative error of at most 0.015.
Values may be sent and summed in bfloat16 or wider, within the bound.
A program may use at most 192 MiB of HBM per device.

v0:
```python
from functools import partial
import jax
import jax.numpy as jnp
from jax import lax
from jax.sharding import PartitionSpec as P

EPSILON = 1e-12
NEGATIVE = -1e30


def gather_feats(shard):
    return lax.all_gather(shard, "col", axis=1, tiled=True)


def back_gather(shard):
    return lax.all_gather(shard, "col", axis=1, tiled=True)


def forward_reduce(partial_rows):
    return lax.psum_scatter(
        partial_rows.astype(jnp.bfloat16), "col", scatter_dimension=1, tiled=True
    ).astype(jnp.float32)


def backward_reduce(partial_rows):
    return lax.psum_scatter(
        partial_rows.astype(jnp.bfloat16), "col", scatter_dimension=1, tiled=True
    ).astype(jnp.float32)


def against(piece_rows, matrix):
    return lax.dot_general(
        piece_rows, matrix, (((1,), (1,)), ((), ())), preferred_element_type=jnp.float32
    )


def column_total(piece_rows):
    unit_row = jnp.ones((1, piece_rows.shape[0]), jnp.bfloat16)
    return jnp.dot(unit_row, piece_rows, preferred_element_type=jnp.float32)[0]


def outer_sum(left_rows, right_rows):
    return lax.dot_general(
        left_rows, right_rows, (((0,), (0,)), ((), ())), preferred_element_type=jnp.float32
    )


def assemble(stacked, row_size, col_size):
    shape = stacked.shape
    grid = stacked.reshape((row_size, col_size) + shape[1:])
    moved = jnp.swapaxes(grid, 1, 2)
    return moved.reshape((row_size * shape[1], col_size * shape[2]) + shape[3:])


def norm_forward(summed, gain, shift, feat_total):
    sum_plain, sum_square = lax.psum(
        (jnp.sum(summed, axis=1), jnp.sum(summed * summed, axis=1)), "col"
    )
    average = sum_plain / feat_total
    inverse = lax.rsqrt(sum_square / feat_total - average * average + EPSILON)
    scaled = (summed - average[:, None]) * inverse[:, None]
    return (scaled * gain + shift, scaled, inverse)


def norm_backward(cotangent, scaled, inverse, gain, feat_total):
    weighted = cotangent * gain
    sum_plain, sum_cross = lax.psum(
        (jnp.sum(weighted, axis=1), jnp.sum(weighted * scaled, axis=1)), "col"
    )
    inner = weighted - sum_plain[:, None] / feat_total - scaled * (sum_cross[:, None] / feat_total)
    return (
        inverse[:, None] * inner,
        jnp.sum(cotangent * scaled, axis=0),
        jnp.sum(cotangent, axis=0),
    )


def visible_rows(token_ids, seq_rows):
    length = token_ids.shape[0]
    memory_rows = (seq_rows - length) // 2
    row_ids = jnp.concatenate(
        [
            jnp.full((memory_rows,), -1, jnp.int32),
            token_ids,
            jnp.full((memory_rows,), length, jnp.int32),
        ]
    )
    return row_ids[None, :] <= row_ids[:, None]


def masked_scores(queries, key_rows, token_ids):
    inv_root = queries.shape[-1] ** (-0.5)
    scores = (
        jnp.einsum("qhe,khe->hqk", queries, key_rows, preferred_element_type=jnp.float32) * inv_root
    )
    visible = visible_rows(token_ids, queries.shape[0])
    return jnp.where(visible[None], scores, NEGATIVE)


def attend(packed):
    queries, key_rows, values, token_ids = packed
    masked = masked_scores(queries, key_rows, token_ids)
    highest = jnp.max(masked, axis=-1, keepdims=True)
    exponent = jnp.exp(masked - highest)
    summed = jnp.sum(exponent, axis=-1, keepdims=True)
    attn_weights = (exponent / summed).astype(jnp.bfloat16)
    mixed_out = jnp.einsum("hqk,khe->qhe", attn_weights, values, preferred_element_type=jnp.float32)
    return (mixed_out.astype(jnp.bfloat16), (highest + jnp.log(summed))[..., 0])


def attend_back(packed):
    queries, key_rows, values, token_ids, log_totals, grad_mixed = packed
    inv_root = queries.shape[-1] ** (-0.5)
    masked = masked_scores(queries, key_rows, token_ids)
    probs_full = jnp.exp(masked - log_totals[..., None])
    attn_weights = probs_full.astype(jnp.bfloat16)
    grad_probs = jnp.einsum("qhe,khe->hqk", grad_mixed, values, preferred_element_type=jnp.float32)
    row_inner = jnp.sum(probs_full * grad_probs, axis=-1, keepdims=True)
    grad_scores = (probs_full * (grad_probs - row_inner)).astype(jnp.bfloat16)
    grad_queries = (
        jnp.einsum("hqk,khe->qhe", grad_scores, key_rows, preferred_element_type=jnp.float32)
        * inv_root
    )
    grad_keys = (
        jnp.einsum("hqk,qhe->khe", grad_scores, queries, preferred_element_type=jnp.float32)
        * inv_root
    )
    grad_values = jnp.einsum(
        "hqk,qhe->khe", attn_weights, grad_mixed, preferred_element_type=jnp.float32
    )
    return (
        grad_queries.astype(jnp.bfloat16),
        grad_keys.astype(jnp.bfloat16),
        grad_values.astype(jnp.bfloat16),
    )


def per_device(
    tokens,
    memory,
    block_ids,
    valid,
    teacher,
    w_qkv,
    bias_qv,
    w_out,
    bias_out,
    ln1_gain,
    ln1_bias,
    w_up,
    bias_up,
    w_down,
    bias_down,
    ln2_gain,
    ln2_bias,
):
    seq_count, feat_cols, length = tokens.shape
    memory_rows = memory.shape[1] // 2
    seq_rows = length + 2 * memory_rows
    row_count = seq_count * seq_rows
    row_size = lax.axis_size("row")
    col_size = lax.axis_size("col")
    row_place = lax.axis_index("row")
    col_place = lax.axis_index("col")
    head_rows = w_qkv.shape[0]
    head_size = bias_qv.shape[1] // 2
    feat_total = feat_cols * col_size
    head_local = head_rows * row_size // col_size
    unit_total = bias_up.shape[0] * row_size
    unit_local = unit_total // col_size
    qkv_blocks = w_qkv.reshape(head_rows, feat_cols, 3 * head_size)
    up_blocks = jnp.transpose(w_up)
    down_blocks = jnp.transpose(w_down)
    whole = (
        lax.all_gather(qkv_blocks[None], ("row", "col"), axis=0, tiled=True),
        lax.all_gather(w_out[None], ("row", "col"), axis=0, tiled=True),
        lax.all_gather(up_blocks[None], ("row", "col"), axis=0, tiled=True),
        lax.all_gather(down_blocks[None], ("row", "col"), axis=0, tiled=True),
    )
    full_qkv = assemble(whole[0], row_size, col_size)
    full_out = assemble(whole[1], row_size, col_size)
    full_up = assemble(whole[2], row_size, col_size)
    full_down = assemble(whole[3], row_size, col_size)
    qkv_heads = lax.dynamic_slice_in_dim(full_qkv, col_place * head_local, head_local, 0)
    out_rows = lax.dynamic_slice_in_dim(
        full_out, col_place * (head_local * head_size), head_local * head_size, 0
    )
    up_rows = lax.dynamic_slice_in_dim(full_up, col_place * unit_local, unit_local, 0)
    down_rows = lax.dynamic_slice_in_dim(full_down, col_place * unit_local, unit_local, 0)
    bias_heads_all, bias_units_all = (
        lax.all_gather(bias_qv, "row", axis=0, tiled=True),
        lax.all_gather(bias_up, "row", axis=0, tiled=True),
    )
    bias_heads = lax.dynamic_slice_in_dim(bias_heads_all, col_place * head_local, head_local, 0)
    bias_units = lax.dynamic_slice_in_dim(bias_units_all, col_place * unit_local, unit_local, 0)
    flat_qkv = jnp.transpose(qkv_heads, (1, 0, 2)).reshape(feat_total, head_local * 3 * head_size)
    token_rows = jnp.swapaxes(tokens, 1, 2)
    inputs = jnp.concatenate(
        [memory[:, :memory_rows], token_rows, memory[:, memory_rows:]], axis=1
    ).reshape(row_count, feat_cols)
    full_in = gather_feats(inputs)
    projected = jnp.dot(full_in, flat_qkv, preferred_element_type=jnp.float32).reshape(
        seq_count, seq_rows, head_local, 3 * head_size
    )
    queries = (projected[..., :head_size] + bias_heads[:, :head_size]).astype(jnp.bfloat16)
    key_rows = projected[..., head_size : 2 * head_size].astype(jnp.bfloat16)
    values = (projected[..., 2 * head_size :] + bias_heads[:, head_size:]).astype(jnp.bfloat16)
    mixed_out, log_totals = lax.map(attend, (queries, key_rows, values, block_ids))
    mixed_rows = mixed_out.reshape(row_count, head_local * head_size)
    attn_out = (
        forward_reduce(jnp.dot(mixed_rows, out_rows, preferred_element_type=jnp.float32)) + bias_out
    )
    norm_one, scaled_one, inverse_one = norm_forward(
        inputs.astype(jnp.float32) + attn_out, ln1_gain, ln1_bias, feat_total
    )
    norm_low = norm_one.astype(jnp.bfloat16)
    full_norm = gather_feats(norm_low)
    gate_pre = against(full_norm, up_rows) + bias_units
    hidden = jax.nn.gelu(gate_pre, approximate=False).astype(jnp.bfloat16)
    branch = (
        forward_reduce(jnp.dot(hidden, down_rows, preferred_element_type=jnp.float32)) + bias_down
    )
    output_rows, scaled_two, inverse_two = norm_forward(
        norm_one + branch, ln2_gain, ln2_bias, feat_total
    )
    output_seq = output_rows.reshape(seq_count, seq_rows, feat_cols)
    offset = lax.axis_index(("dp", "row")) * seq_count
    counts = lax.dynamic_slice_in_dim(valid, offset, seq_count, 0)
    loss_scale = valid.shape[0] * length / jnp.sum(valid).astype(jnp.float32)
    kept_rows = (jnp.arange(length, dtype=jnp.int32)[None, :] < counts[:, None])[..., None]
    mismatch = output_seq[:, memory_rows : memory_rows + length] - jnp.swapaxes(
        teacher, 1, 2
    ).astype(jnp.float32)
    grad_tok = jnp.where(kept_rows, loss_scale * mismatch, 0.0)
    grad_out = jnp.pad(grad_tok, ((0, 0), (memory_rows, memory_rows), (0, 0))).reshape(
        row_count, feat_cols
    )
    grad_two, gain_two, shift_two = norm_backward(
        grad_out, scaled_two, inverse_two, ln2_gain, feat_total
    )
    grad_branch = grad_two.astype(jnp.bfloat16)
    full_branch = back_gather(grad_branch)
    grad_down_rows = outer_sum(hidden, full_branch)
    grad_bias_down = column_total(grad_branch)
    grad_hidden = against(full_branch, down_rows)
    gelu_pull = jax.vjp(partial(jax.nn.gelu, approximate=False), gate_pre)[1]
    grad_gate = gelu_pull(grad_hidden)[0].astype(jnp.bfloat16)
    grad_up_rows = outer_sum(grad_gate, full_norm)
    grad_bias_units = column_total(grad_gate)
    grad_first = grad_two + backward_reduce(
        jnp.dot(grad_gate, up_rows, preferred_element_type=jnp.float32)
    )
    grad_one, gain_one, shift_one = norm_backward(
        grad_first, scaled_one, inverse_one, ln1_gain, feat_total
    )
    grad_attn = grad_one.astype(jnp.bfloat16)
    full_attn = back_gather(grad_attn)
    grad_out_rows = outer_sum(mixed_rows, full_attn)
    grad_bias_out = column_total(grad_attn)
    grad_mixed = against(full_attn, out_rows).astype(jnp.bfloat16)
    grad_mixed = grad_mixed.reshape(seq_count, seq_rows, head_local, head_size)
    grad_queries, grad_keys, grad_values = lax.map(
        attend_back, (queries, key_rows, values, block_ids, log_totals, grad_mixed)
    )
    grad_proj = jnp.concatenate([grad_queries, grad_keys, grad_values], axis=-1).reshape(
        row_count, head_local * 3 * head_size
    )
    grad_flat = outer_sum(full_in, grad_proj).reshape(feat_total, head_local, 3 * head_size)
    grad_heads = jnp.transpose(grad_flat, (1, 0, 2))
    proj_total = column_total(grad_proj).reshape(head_local, 3 * head_size)
    grad_bias_heads = jnp.concatenate(
        [proj_total[:, :head_size], proj_total[:, 2 * head_size :]], axis=1
    )
    grad_in = grad_one + backward_reduce(against(grad_proj, flat_qkv))
    relayed = (
        lax.all_to_all(
            grad_heads.astype(jnp.bfloat16), "col", split_axis=1, concat_axis=0, tiled=True
        ).astype(grad_heads.dtype),
        lax.all_to_all(
            grad_out_rows.astype(jnp.bfloat16), "col", split_axis=1, concat_axis=0, tiled=True
        ).astype(grad_out_rows.dtype),
        lax.all_to_all(
            grad_up_rows.astype(jnp.bfloat16), "col", split_axis=1, concat_axis=0, tiled=True
        ).astype(grad_up_rows.dtype),
        lax.all_to_all(
            grad_down_rows.astype(jnp.bfloat16), "col", split_axis=1, concat_axis=0, tiled=True
        ).astype(grad_down_rows.dtype),
    )
    grid_parts = (
        lax.psum_scatter(
            relayed[0].astype(jnp.bfloat16), "row", scatter_dimension=0, tiled=True
        ).astype(jnp.float32),
        lax.psum_scatter(
            relayed[1].astype(jnp.bfloat16), "row", scatter_dimension=0, tiled=True
        ).astype(jnp.float32),
        lax.psum_scatter(
            relayed[2].astype(jnp.bfloat16), "row", scatter_dimension=0, tiled=True
        ).astype(jnp.float32),
        lax.psum_scatter(
            relayed[3].astype(jnp.bfloat16), "row", scatter_dimension=0, tiled=True
        ).astype(jnp.float32),
    )
    weight_totals = (
        lax.psum(grid_parts[0].astype(jnp.bfloat16), "dp").astype(jnp.float32),
        lax.psum(grid_parts[1].astype(jnp.bfloat16), "dp").astype(jnp.float32),
        lax.psum(grid_parts[2].astype(jnp.bfloat16), "dp").astype(jnp.float32),
        lax.psum(grid_parts[3].astype(jnp.bfloat16), "dp").astype(jnp.float32),
    )
    grad_w_qkv = weight_totals[0].reshape(head_rows, feat_cols * 3 * head_size)
    grad_w_out = weight_totals[1]
    grad_w_up = jnp.transpose(weight_totals[2])
    grad_w_down = jnp.transpose(weight_totals[3])
    heads_pad = lax.dynamic_update_slice_in_dim(
        jnp.zeros((head_local * col_size, 2 * head_size), jnp.float32),
        grad_bias_heads,
        col_place * head_local,
        0,
    )
    units_pad = lax.dynamic_update_slice_in_dim(
        jnp.zeros((unit_total,), jnp.float32), grad_bias_units, col_place * unit_local, 0
    )
    feat_stack = jnp.stack(
        [gain_one, shift_one, gain_two, shift_two, grad_bias_out, grad_bias_down]
    )
    feat_pad = lax.dynamic_update_slice_in_dim(
        jnp.zeros((6, feat_total), jnp.float32), feat_stack, col_place * feat_cols, 1
    )
    small_totals = lax.psum((heads_pad, units_pad, feat_pad), ("dp", "row", "col"))
    grad_bias_qv = lax.dynamic_slice_in_dim(small_totals[0], row_place * head_rows, head_rows, 0)
    grad_bias_up = lax.dynamic_slice_in_dim(
        small_totals[1], row_place * bias_up.shape[0], bias_up.shape[0], 0
    )
    feat_totals = lax.dynamic_slice_in_dim(small_totals[2], col_place * feat_cols, feat_cols, 1)
    grad_seq = grad_in.reshape(seq_count, seq_rows, feat_cols)
    grad_tokens = grad_seq[:, memory_rows : memory_rows + length]
    grad_memory = jnp.concatenate(
        [grad_seq[:, :memory_rows], grad_seq[:, memory_rows + length :]], axis=1
    )
    return (
        output_seq.astype(jnp.bfloat16),
        grad_tokens,
        grad_memory,
        grad_w_qkv,
        grad_bias_qv,
        grad_w_out,
        feat_totals[4],
        feat_totals[0],
        feat_totals[1],
        grad_w_up,
        grad_bias_up,
        grad_w_down,
        feat_totals[5],
        feat_totals[2],
        feat_totals[3],
    )


def solution(mesh):
    in_specs = (
        P(("dp", "row"), "col", None),
        P(("dp", "row"), None, "col"),
        P(("dp", "row"), None),
        P(),
        P(("dp", "row"), "col", None),
        P("row", "col"),
        P("row", None),
        P("row", "col"),
        P("col"),
        P("col"),
        P("col"),
        P("col", "row"),
        P("row"),
        P("col", "row"),
        P("col"),
        P("col"),
        P("col"),
    )
    out_specs = (
        P(("dp", "row"), None, "col"),
        P(("dp", "row"), None, "col"),
        P(("dp", "row"), None, "col"),
        P("row", "col"),
        P("row", None),
        P("row", "col"),
        P("col"),
        P("col"),
        P("col"),
        P("col", "row"),
        P("row"),
        P("col", "row"),
        P("col"),
        P("col"),
        P("col"),
    )
    return jax.shard_map(
        per_device, mesh=mesh, in_specs=in_specs, out_specs=out_specs, check_vma=False
    )
```

profile of v0, /device:TPU:0, one launch (start us, length us, event | category | flops | bytes accessed | tf_op | source)
XLA Modules:
  0.0 976.6 jit_solution(16924794278916850676)
XLA Ops:
  14.5 13.6 %all-gather.3 = f32[4,3,128]{2,1,0:T(4,128)S(1)} all-gather(f32[1,3,128]{2,1,0:T(4,128)S(1)} %bitcast.266), channel_id=1, replica_groups=mesh['dp'=2,'row'=4,'col'=4] {'row'}, dimensions={0}, use_global_device_ids=true | all-gather | bytes 7680 | tf_op jit(solution)/shard_map/all_gather | solution.py:191
  28.2 24.4 %all-gather.24.cloned.1.call-done = bf16[3072,192]{1,0:T(8,128)(2,1)} async-done(((bf16[192,192]{1,0:T(8,128)(2,1)}), bf16[3072,192]{1,0:T(8,128)(2,1)}) %all-gather.24.cloned.1.call-update) | async-done | bytes 1179664 | tf_op jit(solution)/shard_map/all_gather | solution.py:176
  57.5 25.1 %all-gather.14.cloned.1.call-done = bf16[2088,768]{0,1:T(8,128)(2,1)} async-done(((bf16[2088,192]{0,1:T(8,128)(2,1)}), bf16[2088,768]{0,1:T(8,128)(2,1)}) %all-gather.14.cloned.1.call-update) | async-done | bytes 3207184 | tf_op jit(solution)/shard_map/all_gather | solution.py:12
  82.5 8.7 reshape.275
  91.2 47.3 %all-gather.16.cloned.1.call-done = bf16[16,3,192,192]{3,2,1,0:T(8,128)(2,1)} async-done(((bf16[1,3,192,192]{3,2,1,0:T(8,128)(2,1)}), bf16[16,3,192,192]{3,2,1,0:T(8,128)(2,1)}) %all-gather.16.cloned.1.call-update) | async-done | bytes 3538960 | tf_op jit(solution)/shard_map/all_gather | solution.py:175
  138.5 9.7 copy.108
  148.2 7.7 reshape.238
  155.9 4.6 fusion.60
  161.4 51.5 %while.26 = (s32[]{:T(128)}, bf16[2,1044,3,64]{1,3,2,0:T(8,128)(2,1)S(1)}, f32[2,3,1044]{2,1,0:T(4,128)}, bf16[2,1044,3,64]{1,3,2,0:T(8,128)(2,1)S(1)}, s32[2,10...) while((s32[]{:T(128)}, ...), condition=%wide.region_3.4_spmd, body=%wide.region_0.3_spmd.sunk | while | flops 864516608 | bytes 43690424 | solution.py:208
  163.9 8.0 fusion.151
  171.9 7.1 fusion.152
  179.0 7.8 fusion.153
  189.4 8.0 fusion.151
  197.4 7.1 fusion.152
  204.5 7.8 fusion.153
  218.0 4.0 convolution_convert_fusion.3
  223.5 36.4 %reduce-scatter.9.cloned.1.call-done = bf16[2088,192]{0,1:T(8,128)(2,1)} async-done(((bf16[2088,768]{0,1:T(8,128)(2,1)}), bf16[2088,192]{0,1:T(8,128)(2,1)}) %reduce-scatter.9.cloned.1.call-update) | async-done | bytes 801808 | tf_op jit(solution)/shard_map/reduce_scatter | solution.py:20
  261.6 10.3 %all-reduce.5 = (f32[2088]{0:T(1024)S(1)}, f32[2088]{0:T(1024)S(1)}) all-reduce(f32[2088]{0:T(1024)S(1)} %get-tuple-element.158, f32[2088]{0:T(1024)S(1)} %get-tuple-element.157), channel_id=1, replica_groups=mesh['dp'=2,'row'=4,'col'=4] {'col'}, use_global_device_ids=true, to_apply=%region_8.9 | all-reduce | flops 4176 | bytes 33408 | tf_op jit(solution)/shard_map/psum | solution.py:56
  274.6 13.3 %all-gather.4 = f32[4,1,768]{2,1,0:T(1,128)S(1)} all-gather(f32[1,1,768]{2,1,0:T(1,128)S(1)} %reshape.262), channel_id=1, replica_groups=mesh['dp'=2,'row'=4,'col'=4] {'row'}, dimensions={0}, use_global_device_ids=true | all-gather | bytes 15360 | tf_op jit(solution)/shard_map/all_gather | solution.py:192
  288.0 27.5 %all-gather.26.cloned.1.call-done = bf16[12288,192]{0,1:T(8,128)(2,1)} async-done(((bf16[768,192]{0,1:T(8,128)(2,1)}), bf16[12288,192]{0,1:T(8,128)(2,1)}) %all-gather.26.cloned.1.call-update) | async-done | bytes 4718608 | tf_op jit(solution)/shard_map/all_gather | solution.py:177
  315.5 8.2 reshape.243
  323.7 4.3 copy.111
  328.0 3.2 copy.143
  331.2 38.2 %all-gather.28.cloned.1.call-done = bf16[12288,192]{0,1:T(8,128)(2,1)} async-done(((bf16[768,192]{0,1:T(8,128)(2,1)}), bf16[12288,192]{0,1:T(8,128)(2,1)}) %all-gather.28.cloned.1.call-update) | async-done | bytes 4718608 | tf_op jit(solution)/shard_map/all_gather | solution.py:178
  369.4 8.3 reshape.245
  377.7 4.7 copy.112
  385.5 14.0 %all-gather.18.cloned.1.call-done = bf16[2088,768]{0,1:T(8,128)(2,1)} async-done(((bf16[2088,192]{0,1:T(8,128)(2,1)}), bf16[2088,768]{0,1:T(8,128)(2,1)}) %all-gather.18.cloned.1.call-update) | async-done | bytes 3207184 | tf_op jit(solution)/shard_map/all_gather | solution.py:12
  399.5 20.0 %multiply_convert_fusion.1 = (bf16[2088,768]{1,0:T(8,128)(2,1)S(1)}, f32[2088,768]{1,0:T(8,128)}, f32[2088,768]{1,0:T(8,128)}) fusion(f32[768]{0:T(1024)S(1)} %dynamic_slice.67, bf16[2088,768]{0,1:T(8,128)(2,1)} %all-gather.18.cloned.1.call-done, bf16[3072,768]{0,1:T(8,128)(2,1)} %bitcast.237, s32[]{:T(128)S(6)} %select_n.38), kind=kOutput, calls=%fused_computation.65 | convolution fusion | flops 2568941568 | bytes 20560900 | tf_op jit(solution)/shard_map/dot_general | solution.py:32
  421.2 5.9 convolution_convert_fusion.2
  429.2 37.2 %reduce-scatter.11.cloned.1.call-done = bf16[2088,192]{0,1:T(8,128)(2,1)} async-done(((bf16[2088,768]{0,1:T(8,128)(2,1)}), bf16[2088,192]{0,1:T(8,128)(2,1)}) %reduce-scatter.11.cloned.1.call-update) | async-done | bytes 801808 | tf_op jit(solution)/shard_map/reduce_scatter | solution.py:20
  468.7 10.6 %all-reduce.4 = (f32[2088]{0:T(1024)S(1)}, f32[2088]{0:T(1024)S(1)}) all-reduce(f32[2088]{0:T(1024)S(1)} %get-tuple-element.161, f32[2088]{0:T(1024)S(1)} %get-tuple-element.160), channel_id=1, replica_groups=mesh['dp'=2,'row'=4,'col'=4] {'col'}, use_global_device_ids=true, to_apply=%region_13.14 | all-reduce | flops 4176 | bytes 33408 | tf_op jit(solution)/shard_map/psum | solution.py:56
  480.9 3.5 reshape.247
  490.3 4.5 pad.4.clone
  494.8 3.2 reshape.248
  500.5 10.3 %all-reduce.3 = (f32[2088]{0:T(1024)S(1)}, f32[2088]{0:T(1024)S(1)}) all-reduce(f32[2088]{0:T(1024)S(1)} %get-tuple-element.155, f32[2088]{0:T(1024)S(1)} %reduce_sum.143), channel_id=1, replica_groups=mesh['dp'=2,'row'=4,'col'=4] {'col'}, use_global_device_ids=true, to_apply=%region_18.19 | all-reduce | flops 4176 | bytes 33408 | tf_op jit(solution)/shard_map/psum | solution.py:67
  514.1 29.9 %all-gather.20.cloned.1.call-done = bf16[2088,768]{0,1:T(8,128)(2,1)} async-done(((bf16[2088,192]{0,1:T(8,128)(2,1)}), bf16[2088,768]{0,1:T(8,128)(2,1)}) %all-gather.20.cloned.1.call-update) | async-done | bytes 3207184 | tf_op jit(solution)/shard_map/all_gather | solution.py:16
  544.0 10.5 %add_convert_fusion = bf16[2088,768]{1,0:T(8,128)(2,1)S(1)} fusion(f32[2088,768]{1,0:T(8,128)} %get-tuple-element.216, f32[2088,768]{1,0:T(8,128)} %get-tuple-element.241, bf16[2088,768]{0,1:T(8,128)(2,1)} %all-gather.20.cloned.1.call-done, bf16[3072,768]{0,1:T(8,128)(2,1)} %bitcast.240, s32[]{:T(128)S(6)} %select_n.38), kind=kOutput, calls=%fused_computation.64 | convolution fusion | flops 2485555200 | bytes 20557828 | tf_op jit(solution)/shard_map/dot_general | solution.py:32
  556.2 6.0 convolution_convert_fusion.1
  562.3 39.2 %reduce-scatter.13.cloned.1.call-done = bf16[2088,192]{0,1:T(8,128)(2,1)} async-done(((bf16[2088,768]{0,1:T(8,128)(2,1)}), bf16[2088,192]{0,1:T(8,128)(2,1)}) %reduce-scatter.13.cloned.1.call-update) | async-done | bytes 801808 | tf_op jit(solution)/shard_map/reduce_scatter | solution.py:26
  601.5 5.0 multiply_reduce_fusion.3
  606.5 10.3 %all-reduce.2 = (f32[2088]{0:T(1024)S(1)}, f32[2088]{0:T(1024)S(1)}) all-reduce(f32[2088]{0:T(1024)S(1)} %get-tuple-element.153, f32[2088]{0:T(1024)S(1)} %get-tuple-element.156), channel_id=1, replica_groups=mesh['dp'=2,'row'=4,'col'=4] {'col'}, use_global_device_ids=true, to_apply=%region_23.24 | all-reduce | flops 4176 | bytes 33408 | tf_op jit(solution)/shard_map/psum | solution.py:67
  620.3 30.1 %all-gather.22.cloned.1.call-done = bf16[2088,768]{0,1:T(8,128)(2,1)} async-done(((bf16[2088,192]{0,1:T(8,128)(2,1)}), bf16[2088,768]{0,1:T(8,128)(2,1)}) %all-gather.22.cloned.1.call-update) | async-done | bytes 3207184 | tf_op jit(solution)/shard_map/all_gather | solution.py:16
  650.4 3.7 convolution_convert_fusion.4
  660.9 68.2 %while.27 = (s32[]{:T(128)}, bf16[2,1044,3,64]{1,3,2,0:T(8,128)(2,1)}, bf16[2,1044,3,64]{1,3,2,0:T(8,128)(2,1)}, bf16[2,1044,3,64]{1,3,2,0:T(8,128)(2,1)}, bf16[...) while((s32[]{:T(128)}, ...), condition=%wide.region_26.27_spmd, body=%wide.region_24.26_spmd.sunk | while | flops 2124194560 | bytes 151329200 | solution.py:262
  661.8 3.4 fusion.162
  665.2 8.2 multiply_reduce_fusion.10
  673.5 8.6 multiply_convert_fusion.3
  682.1 8.3 fusion.165
  695.8 3.4 fusion.162
  699.2 8.2 multiply_reduce_fusion.10
  707.5 8.6 multiply_convert_fusion.3
  716.0 8.3 fusion.165
  736.8 5.0 fusion.72
  742.7 22.5 %all_to_all.75 = bf16[3,768,192]{2,0,1:T(4,128)(2,1)S(1)} all-to-all(bf16[3,768,192]{2,0,1:T(4,128)(2,1)S(1)} %copy.121), channel_id=1, replica_groups=mesh['dp'=2,'row'=4,'col'=4] {'col'}, dimensions={1} | all-to-all | bytes 1769472 | tf_op jit(solution)/shard_map/all_to_all | solution.py:276
  767.6 4.8 convolution_convert_fusion.5
  772.4 18.5 %all_to_all.76 = bf16[768,4,192]{0,2,1:T(8,128)(2,1)S(1)} all-to-all(bf16[768,4,192]{0,2,1:T(8,128)(2,1)S(1)} %bitcast.250), channel_id=1, replica_groups=mesh['dp'=2,'row'=4,'col'=4] {'col'}, dimensions={1} | all-to-all | bytes 2359296 | tf_op jit(solution)/shard_map/all_to_all | solution.py:285
  792.2 4.9 convolution_convert_fusion.6
  797.1 18.4 %all_to_all.77 = bf16[768,4,192]{0,2,1:T(8,128)(2,1)S(1)} all-to-all(bf16[768,4,192]{0,2,1:T(8,128)(2,1)S(1)} %bitcast.251), channel_id=1, replica_groups=mesh['dp'=2,'row'=4,'col'=4] {'col'}, dimensions={1} | all-to-all | bytes 2359296 | tf_op jit(solution)/shard_map/all_to_all | solution.py:282
  820.7 10.6 %all_to_all.78 = bf16[192,4,192]{2,0,1:T(8,128)(2,1)} all-to-all(bf16[192,4,192]{2,0,1:T(8,128)(2,1)S(1)} %copy.124), channel_id=1, replica_groups=mesh['dp'=2,'row'=4,'col'=4] {'col'}, dimensions={1} | all-to-all | bytes 589824 | tf_op jit(solution)/shard_map/all_to_all | solution.py:279
  833.5 22.8 %reduce-scatter.21.cloned.1.call-done = bf16[768,192]{0,1:T(8,128)(2,1)} async-done(((bf16[3072,192]{0,1:T(8,128)(2,1)}), bf16[768,192]{0,1:T(8,128)(2,1)}) %reduce-scatter.21.cloned.1.call-update) | async-done | bytes 294928 | tf_op jit(solution)/shard_map/reduce_scatter | solution.py:296
  856.3 21.5 %reduce-scatter.19.cloned.1.call-done = bf16[192,192]{1,0:T(8,128)(2,1)} async-done(((bf16[768,192]{1,0:T(8,128)(2,1)}), bf16[192,192]{1,0:T(8,128)(2,1)}) %reduce-scatter.19.cloned.1.call-update) | async-done | bytes 73744 | tf_op jit(solution)/shard_map/reduce_scatter | solution.py:293
  877.9 5.8 convolution_convert_fusion
  893.4 39.6 %all-reduce.1 = (f32[12,128]{1,0:T(8,128)S(1)}, f32[6,768]{1,0:T(8,128)S(1)}, f32[3072]{0:T(1024)S(1)}) all-reduce(f32[12,128]{1,0:T(8,128)S(1)} %dynamic_update_slice.26, f32[6,768]{1,0:T(8,128)S(1)} %dynamic_update_slice.27, f32[3072]{0:T(1024)S(1)} %dynamic_update_slice.28), channel_id=1, replica_groups=mesh['dp'=2,'row'=4,'col'=4] {'dp','row','col'}, use_global_device_ids=true, to_apply=%region_30.31 | all-reduce | flops 9216 | bytes 73728 | tf_op jit(solution)/shard_map/psum | solution.py:328
  942.1 17.5 %reduce-scatter.15.cloned.1.call-done = bf16[2088,192]{0,1:T(8,128)(2,1)} async-done(((bf16[2088,768]{0,1:T(8,128)(2,1)}), bf16[2088,192]{0,1:T(8,128)(2,1)}) %reduce-scatter.15.cloned.1.call-update) | async-done | bytes 801808 | tf_op jit(solution)/shard_map/reduce_scatter | solution.py:26
  (285 shorter events, 122.0 us)
Async XLA Ops:
  7.2 45.4 %all-gather.24.cloned.1.call-start = ((), (), s32[]{:S(2)}) async-start(), calls=%async_computation.25 | async-start | bytes 1671168 | tf_op jit(solution)/shard_map/all_gather | solution.py:176
  7.9 74.6 %all-gather.14.cloned.1.call-start = ((), (), s32[]{:S(2)}) async-start(), calls=%async_computation.12 | async-start | bytes 4177920 | tf_op jit(solution)/shard_map/all_gather | solution.py:12
  8.7 4.6 copy-start.30
  9.0 5.5 copy-start.51
  13.3 125.2 %all-gather.16.cloned.1.call-start = ((), (), s32[]{:S(2)}) async-start(), calls=%async_computation.13 | async-start | bytes 5013504 | tf_op jit(solution)/shard_map/all_gather | solution.py:175
  14.4 245.5 %reduce-scatter.9.cloned.1.call-start = ((), (), s32[]{:S(2)}) async-start(), calls=%async_computation.14 | async-start | bytes 4177920 | tf_op jit(solution)/shard_map/reduce_scatter | solution.py:20
  155.9 4.7 copy-start.24
  179.0 7.8 copy-start.31
  179.0 8.4 copy-start.35
  204.5 7.8 copy-start.31
  204.5 8.4 copy-start.35
  212.9 5.1 copy-start.3
  212.9 9.1 copy-start.5
  222.0 37.9 %copy-start.1 = (bf16[2088,192]{0,1:T(8,128)(2,1)S(1)}, bf16[2088,192]{0,1:T(8,128)(2,1)}, u32[]{:S(2)}) copy-start(bf16[2088,192]{0,1:T(8,128)(2,1)} %reshape.236) | copy-start | bytes 2405380
  222.0 37.9 %copy-start.40 = (f32[192]{0:T(256)S(1)}, f32[192]{0:T(256)}, u32[]{:S(2)}) copy-start(f32[192]{0:T(256)} %param.29) | copy-start | bytes 2308
  222.1 49.8 %copy-start.43 = (f32[192]{0:T(256)S(1)}, f32[192]{0:T(256)}, u32[]{:S(2)}) copy-start(f32[192]{0:T(256)} %param.30) | copy-start | bytes 2308
  222.1 49.8 %copy-start.45 = (f32[192]{0:T(256)S(1)}, f32[192]{0:T(256)}, u32[]{:S(2)}) copy-start(f32[192]{0:T(256)} %param.31) | copy-start | bytes 2308
  222.1 52.5 %copy-start.49 = (f32[768]{0:T(1024)S(1)}, f32[768]{0:T(1024)}, u32[]{:S(2)}) copy-start(f32[768]{0:T(1024)} %param.33) | copy-start | bytes 9220
  222.1 93.4 %all-gather.26.cloned.1.call-start = ((), (), s32[]{:S(2)}) async-start(), calls=%async_computation.26 | async-start | bytes 5013504 | tf_op jit(solution)/shard_map/all_gather | solution.py:177
  222.7 146.7 %all-gather.28.cloned.1.call-start = ((), (), s32[]{:S(2)}) async-start(), calls=%async_computation.27 | async-start | bytes 5013504 | tf_op jit(solution)/shard_map/all_gather | solution.py:178
  223.3 176.3 %all-gather.18.cloned.1.call-start = ((), (), s32[]{:S(2)}) async-start(), calls=%async_computation.15 | async-start | bytes 4177920 | tf_op jit(solution)/shard_map/all_gather | solution.py:12
  271.9 345.0 %copy-start.26 = (f32[2088]{0:T(1024)}, f32[2088]{0:T(1024)S(1)}, u32[]{:S(2)}) copy-start(f32[2088]{0:T(1024)S(1)} %get-tuple-element.235) | copy-start | bytes 25060
  271.9 345.0 %copy-start.28 = (f32[2088]{0:T(1024)}, f32[2088]{0:T(1024)S(1)}, u32[]{:S(2)}) copy-start(f32[2088]{0:T(1024)S(1)} %get-tuple-element.236) | copy-start | bytes 25060
  274.6 191.9 %reduce-scatter.11.cloned.1.call-start = ((), (), s32[]{:S(2)}) async-start(), calls=%async_computation.16 | async-start | bytes 4177920 | tf_op jit(solution)/shard_map/reduce_scatter | solution.py:20
  427.1 39.3 %copy-start.8 = (bf16[2088,192]{0,1:T(8,128)(2,1)S(1)}, bf16[2088,192]{0,1:T(8,128)(2,1)}, u32[]{:S(2)}) copy-start(bf16[2088,192]{0,1:T(8,128)(2,1)} %reduce-scatter.9.cloned.1.call-done) | copy-start | bytes 2405380
  427.1 39.3 %copy-start.52 = (f32[192]{0:T(256)S(1)}, f32[192]{0:T(256)}, u32[]{:S(2)}) copy-start(f32[192]{0:T(256)} %param.35) | copy-start | bytes 2308
  427.1 52.2 %copy-start.42 = (f32[192]{0:T(256)S(1)}, f32[192]{0:T(256)}, u32[]{:S(2)}) copy-start(f32[192]{0:T(256)} %param.36) | copy-start | bytes 2308
  427.1 52.2 %copy-start.53 = (f32[192]{0:T(256)S(1)}, f32[192]{0:T(256)}, u32[]{:S(2)}) copy-start(f32[192]{0:T(256)} %param.37) | copy-start | bytes 2308
  427.2 116.8 %all-gather.20.cloned.1.call-start = ((), (), s32[]{:S(2)}) async-start(), calls=%async_computation.17 | async-start | bytes 4177920 | tf_op jit(solution)/shard_map/all_gather | solution.py:16
  513.6 87.9 %reduce-scatter.13.cloned.1.call-start = ((), (), s32[]{:S(2)}) async-start(), calls=%async_computation.18 | async-start | bytes 4177920 | tf_op jit(solution)/shard_map/reduce_scatter | solution.py:26
  562.2 88.1 %all-gather.22.cloned.1.call-start = ((), (), s32[]{:S(2)}) async-start(), calls=%async_computation.19 | async-start | bytes 4177920 | tf_op jit(solution)/shard_map/all_gather | solution.py:16
  616.8 37.3 %copy-start.36 = (f32[2088]{0:T(1024)}, f32[2088]{0:T(1024)S(1)}, u32[]{:S(2)}) copy-start(f32[2088]{0:T(1024)S(1)} %broadcast_multiply_fusion) | copy-start | bytes 25060
  616.8 37.3 %copy-start.38 = (f32[2088]{0:T(1024)}, f32[2088]{0:T(1024)S(1)}, u32[]{:S(2)}) copy-start(f32[2088]{0:T(1024)S(1)} %broadcast_multiply_fusion.1) | copy-start | bytes 25060
  620.0 211.4 %reduce-scatter.17.cloned.1.call-start = ((), (), s32[]{:S(2)}) async-start(), calls=%async_computation.21 | async-start | bytes 1474560 | tf_op jit(solution)/shard_map/reduce_scatter | solution.py:290
  654.1 6.8 copy-start.4
  654.1 6.8 copy-start.6
  654.1 6.8 copy-start.33
  673.5 8.6 copy-start.7
  682.0 8.3 copy-start
  682.0 8.3 copy-start.17
  707.5 8.6 copy-start.7
  716.0 8.3 copy-start
  716.0 8.3 copy-start.17
  766.5 67.0 %reduce-scatter.23.cloned.1.call-start = ((), (), s32[]{:S(2)}) async-start(), calls=%async_computation.24 | async-start | bytes 1474560 | tf_op jit(solution)/shard_map/reduce_scatter | solution.py:299
  772.4 19.8 %copy-start.22 = (bf16[2088,768]{1,0:T(8,128)(2,1)S(1)}, bf16[2088,768]{1,0:T(8,128)(2,1)}, u32[]{:S(2)}) copy-start(bf16[2088,768]{1,0:T(8,128)(2,1)} %copy-done.21) | copy-start | bytes 9621508
  792.2 64.2 %reduce-scatter.21.cloned.1.call-start = ((), (), s32[]{:S(2)}) async-start(), calls=%async_computation.23 | async-start | bytes 1474560 | tf_op jit(solution)/shard_map/reduce_scatter | solution.py:296
  797.1 20.1 %copy-start.13 = (bf16[2088,192]{0,1:T(8,128)(2,1)S(1)}, bf16[2088,192]{0,1:T(8,128)(2,1)}, u32[]{:S(2)}) copy-start(bf16[2088,192]{0,1:T(8,128)(2,1)} %copy-done.12) | copy-start | bytes 2405380
  816.7 61.1 %reduce-scatter.19.cloned.1.call-start = ((), (), s32[]{:S(2)}) async-start(), calls=%async_computation.22 | async-start | bytes 491520 | tf_op jit(solution)/shard_map/reduce_scatter | solution.py:293
  820.3 57.6 %copy-start.15 = (bf16[2088,576]{0,1:T(8,128)(2,1)S(1)}, bf16[2088,576]{0,1:T(8,128)(2,1)}, u32[]{:S(2)}) copy-start(bf16[2088,576]{0,1:T(8,128)(2,1)} %reshape.250) | copy-start | bytes 7216132
  831.4 103.6 %all-reduce.9.cloned.1.call-start = ((), (), s32[]{:S(2)}) async-start(), calls=%async_computation.28 | async-start | bytes 1966080 | tf_op jit(solution)/shard_map/psum | solution.py:304
  877.9 81.7 %reduce-scatter.15.cloned.1.call-start = ((), (), s32[]{:S(2)}) async-start(), calls=%async_computation.20 | async-start | bytes 4177920 | tf_op jit(solution)/shard_map/reduce_scatter | solution.py:26
  885.5 4.8 copy-start.46
  885.5 4.8 copy-start.47
  885.5 4.9 copy-start.48
  885.5 4.9 copy-start.50
  888.6 70.9 %copy-start.2 = (bf16[2088,192]{0,1:T(8,128)(2,1)S(1)}, bf16[2088,192]{0,1:T(8,128)(2,1)}, u32[]{:S(2)}) copy-start(bf16[2088,192]{0,1:T(8,128)(2,1)} %reshape.236) | copy-start | bytes 2405380
  888.6 70.9 %copy-start.9 = (bf16[2088,192]{0,1:T(8,128)(2,1)S(1)}, bf16[2088,192]{0,1:T(8,128)(2,1)}, u32[]{:S(2)}) copy-start(bf16[2088,192]{0,1:T(8,128)(2,1)} %reduce-scatter.9.cloned.1.call-done) | copy-start | bytes 2405380
  888.6 70.9 %copy-start.11 = (f32[2088,192]{0,1:T(8,128)S(1)}, f32[2088,192]{0,1:T(8,128)}, u32[]{:S(2)}) copy-start(f32[2088,192]{0,1:T(8,128)} %get-tuple-element.213) | copy-start | bytes 4810756
  888.6 70.9 %copy-start.27 = (f32[2088]{0:T(1024)S(1)}, f32[2088]{0:T(1024)}, u32[]{:S(2)}) copy-start(f32[2088]{0:T(1024)} %copy-done.26) | copy-start | bytes 25060
  888.6 70.9 %copy-start.29 = (f32[2088]{0:T(1024)S(1)}, f32[2088]{0:T(1024)}, u32[]{:S(2)}) copy-start(f32[2088]{0:T(1024)} %copy-done.28) | copy-start | bytes 25060
  888.6 70.9 %copy-start.37 = (f32[2088]{0:T(1024)S(1)}, f32[2088]{0:T(1024)}, u32[]{:S(2)}) copy-start(f32[2088]{0:T(1024)} %copy-done.36) | copy-start | bytes 25060
  888.7 70.9 %copy-start.39 = (f32[2088]{0:T(1024)S(1)}, f32[2088]{0:T(1024)}, u32[]{:S(2)}) copy-start(f32[2088]{0:T(1024)} %copy-done.38) | copy-start | bytes 25060
  888.7 70.9 %copy-start.41 = (f32[192]{0:T(256)S(1)}, f32[192]{0:T(256)}, u32[]{:S(2)}) copy-start(f32[192]{0:T(256)} %param.29) | copy-start | bytes 2308
  888.7 70.9 %copy-start.44 = (f32[192]{0:T(256)S(1)}, f32[192]{0:T(256)}, u32[]{:S(2)}) copy-start(f32[192]{0:T(256)} %param.30) | copy-start | bytes 2308
  (19 other events, 30.9 us)
Sparse Core Ops, SparseCore 0:
  10.3 42.2 all-gather.23
  54.2 28.3 all-gather.13
  85.4 53.1 all-gather.15
  222.2 37.6 reduce-scatter.8
  262.0 53.4 all-gather.25
  317.6 51.7 all-gather.27
  371.5 27.9 all-gather.17
  427.3 39.0 reduce-scatter.10
  513.7 30.2 all-gather.19
  562.3 39.1 reduce-scatter.12
  620.2 30.1 all-gather.21
  766.6 29.3 reduce-scatter.16
  798.3 27.9 reduce-scatter.22
  828.4 27.9 reduce-scatter.20
  858.5 19.3 reduce-scatter.18
  880.8 37.2 all-reduce.8
  920.5 39.0 reduce-scatter.14
where the time goes:
time: 987 us; the launch traced here: 977 us
  waiting for transfers between devices  413 us (42%)
  blocking collectives  178 us (18%)
  matrix products  162 us (16%)
  local copies, waits for them, and re-layouts  134 us (14%)
  other arithmetic  71.6 us (7%)
  between operations  15.7 us (2%)
    reduce_scatter x2, waiting for transfers between devices, forward_reduce(): lax.psum_scatter(partial_rows.astype(jnp.bfloat16), 'col', scatter_dimens...  73.6 us
    all_gather x2, waiting for transfers between devices, back_gather(): return lax.all_gather(shard, 'col', axis=1, tiled=True)  60 us
    reduce_scatter x2, waiting for transfers between devices, backward_reduce(): lax.psum_scatter(partial_rows.astype(jnp.bfloat16), 'col', scatter_dimens...  56.7 us
    all_gather x1, waiting for transfers between devices, per_device(): lax.all_gather(qkv_blocks[None], ('row', 'col'), axis=0, tiled=True)  47.3 us
    dot_general x4, matrix products, against(): lax.dot_general(piece_rows, matrix, (((1,), (1,)), ((), ())), preferred_e...  40 us
    psum x1, blocking collectives, per_device(): lax.psum((heads_pad, units_pad, feat_pad), ('dp', 'row', 'col'))  39.6 us
    all_gather x2, waiting for transfers between devices, gather_feats(): return lax.all_gather(shard, 'col', axis=1, tiled=True)  39.1 us
    all_gather x1, waiting for transfers between devices, per_device(): lax.all_gather(down_blocks[None], ('row', 'col'), axis=0, tiled=True)  38.2 us
  transfers between devices with their start and end apart: 17, of which 14 were waited for; matrix products, arithmetic and copies ran while one was open for 10% of the time, Pallas kernels for 0%

commit v1 on v0

--- a/solution.py
+++ b/solution.py
@@ -6,6 +6,18 @@
 
 EPSILON = 1e-12
 NEGATIVE = -1e30
+
+
+def doubled_up(x, axis, dim):
+    ways, here = (lax.axis_size(axis), lax.axis_index(axis))
+    grown, reach = (x, 1)
+    while reach < ways:
+        theirs = lax.ppermute(grown, axis, [(d, d ^ reach) for d in range(ways)])
+        mine_first = jnp.concatenate([grown, theirs], axis=dim)
+        theirs_first = jnp.concatenate([theirs, grown], axis=dim)
+        grown = jnp.where(here & reach == 0, mine_first, theirs_first)
+        reach = 2 * reach
+    return grown
 
 
 def gather_feats(shard):
@@ -172,7 +184,7 @@
     up_blocks = jnp.transpose(w_up)
     down_blocks = jnp.transpose(w_down)
     whole = (
-        lax.all_gather(qkv_blocks[None], ("row", "col"), axis=0, tiled=True),
+        doubled_up(qkv_blocks[None], ("row", "col"), 0),
         lax.all_gather(w_out[None], ("row", "col"), axis=0, tiled=True),
         lax.all_gather(up_blocks[None], ("row", "col"), axis=0, tiled=True),
         lax.all_gather(down_blocks[None], ("row", "col"), axis=0, tiled=True),

time: 987 us -> 1050 us (1.064)
  blocking collectives: 178 us -> 272 us
  waiting for transfers between devices: 413 us -> 364 us
    all_gather x1, blocking collectives: 13.6 us -> 108 us  [per_device(): lax.all_gather(bias_qv, 'row', axis=0, tiled=True)]
    ppermute x0 -> x4, waiting for transfers between devices: none -> 48 us  [doubled_up(): theirs = lax.ppermute(grown, axis, [(d, d ^ reach) for d in range(ways)])]
    all_gather x1 -> x0, waiting for transfers between devices: 47.3 us -> none  [per_device(): lax.all_gather(qkv_blocks[None], ('row', 'col'), axis=0, tiled=True)]
    all_gather x2, waiting for transfers between devices: 39.1 us -> 14 us  [gather_feats(): return lax.all_gather(shard, 'col', axis=1, tiled=True)]
    all_gather x1, waiting for transfers between devices: 24.4 us -> 0.01 us  [per_device(): lax.all_gather(w_out[None], ('row', 'col'), axis=0, tiled=True)]
    reshape x6 -> x5, local copies, waits for them, and re-layouts: 37.7 us -> 29.1 us  [assemble(): grid = stacked.reshape((row_size, col_size) + shape[1:])]
  transfers between devices with their start and end apart: 17 -> 20, of which waited for: 14 -> 14; matrix products, arithmetic and copies ran while one was open for 10% -> 11% of each run, Pallas kernels for 0% -> 0%
where the time goes in v1:
time: 1050 us; the launch traced here: 1040 us
  waiting for transfers between devices  364 us (35%)
  blocking collectives  272 us (26%)
  matrix products  161 us (15%)
  local copies, waits for them, and re-layouts  135 us (13%)
  other arithmetic  80.5 us (8%)
  between operations  15.6 us (1%)
    all_gather x1, blocking collectives, per_device(): lax.all_gather(bias_qv, 'row', axis=0, tiled=True)  108 us
    reduce_scatter x2, waiting for transfers between devices, forward_reduce(): lax.psum_scatter(partial_rows.astype(jnp.bfloat16), 'col', scatter_dimens...  73.3 us
    all_gather x2, waiting for transfers between devices, back_gather(): return lax.all_gather(shard, 'col', axis=1, tiled=True)  60 us
    reduce_scatter x2, waiting for transfers between devices, backward_reduce(): lax.psum_scatter(partial_rows.astype(jnp.bfloat16), 'col', scatter_dimens...  56.7 us
    ppermute x4, waiting for transfers between devices, doubled_up(): theirs = lax.ppermute(grown, axis, [(d, d ^ reach) for d in range(ways)])  48 us
    dot_general x4, matrix products, against(): lax.dot_general(piece_rows, matrix, (((1,), (1,)), ((), ())), preferred_e...  40.1 us
    psum x1, blocking collectives, per_device(): lax.psum((heads_pad, units_pad, feat_pad), ('dp', 'row', 'col'))  39.6 us
    all_gather x1, waiting for transfers between devices, per_device(): lax.all_gather(down_blocks[None], ('row', 'col'), axis=0, tiled=True)  38.2 us
  transfers between devices with their start and end apart: 20, of which 14 were waited for; matrix products, arithmetic and copies ran while one was open for 11% of the time, Pallas kernels for 0%

profile of v1, /device:TPU:0, one launch (start us, length us, event | category | flops | bytes accessed | tf_op | source)
XLA Modules:
  0.0 1039.3 jit_solution(1490568451127423214)
XLA Ops:
  18.6 14.7 %collective-permute-done.1 = bf16[2,3,192,192]{3,2,1,0:T(8,128)(2,1)S(1)} collective-permute-done((bf16[2,3,192,192]{3,2,1,0:T(8,128)(2,1)S(1)}, bf16[2,3,192,192]{3,2,1,0:T(8,128)(2,1)S(1)}, u32[]{:S(2)}, u32[]{:S(2)}) %collective-permute-start.1) | collective-permute-done | bytes 442400 | tf_op jit(solution)/shard_map/ppermute | solution.py:15
  35.5 32.1 %collective-permute-done.2 = bf16[4,3,192,192]{3,2,1,0:T(8,128)(2,1)} collective-permute-done((bf16[4,3,192,192]{3,2,1,0:T(8,128)(2,1)S(1)}, bf16[4,3,192,192]{3,2,1,0:T(8,128)(2,1)}, u32[]{:S(2)}, u32[]{:S(2)}) %collective-permute-start.2) | collective-permute-done | bytes 884768 | tf_op jit(solution)/shard_map/ppermute | solution.py:15
  72.3 107.9 %all-gather.3 = f32[4,3,128]{2,1,0:T(4,128)S(1)} all-gather(f32[1,3,128]{2,1,0:T(4,128)S(1)} %bitcast.266), channel_id=1, replica_groups=mesh['dp'=2,'row'=4,'col'=4] {'row'}, dimensions={0}, use_global_device_ids=true | all-gather | bytes 7680 | tf_op jit(solution)/shard_map/all_gather | solution.py:203
  180.3 3.8 copy.153
  184.1 4.0 reshape.243
  188.1 6.3 maximum_select_fusion
  194.4 9.7 copy.109
  204.1 7.7 reshape.239
  212.7 7.4 reshape.276
  220.1 3.5 fusion.60
  224.5 51.6 %while.26 = (s32[]{:T(128)}, bf16[2,1044,3,64]{1,3,2,0:T(8,128)(2,1)S(1)}, f32[2,3,1044]{2,1,0:T(4,128)}, bf16[2,1044,3,64]{1,3,2,0:T(8,128)(2,1)S(1)}, s32[2,10...) while((s32[]{:T(128)}, ...), condition=%wide.region_3.4_spmd, body=%wide.region_0.3_spmd.sunk | while | flops 864516608 | bytes 43690424 | solution.py:220
  227.0 8.0 fusion.151
  235.0 7.1 fusion.152
  242.1 7.8 fusion.153
  252.5 8.0 fusion.151
  260.5 7.1 fusion.152
  267.6 7.8 fusion.153
  281.1 4.1 convolution_convert_fusion.3
  286.7 36.1 %reduce-scatter.9.cloned.1.call-done = bf16[2088,192]{0,1:T(8,128)(2,1)} async-done(((bf16[2088,768]{0,1:T(8,128)(2,1)}), bf16[2088,192]{0,1:T(8,128)(2,1)}) %reduce-scatter.9.cloned.1.call-update) | async-done | bytes 801808 | tf_op jit(solution)/shard_map/reduce_scatter | solution.py:32
  324.4 10.3 all-reduce.5
  337.4 13.3 %all-gather.4 = f32[4,1,768]{2,1,0:T(1,128)S(1)} all-gather(f32[1,1,768]{2,1,0:T(1,128)S(1)} %reshape.263), channel_id=1, replica_groups=mesh['dp'=2,'row'=4,'col'=4] {'row'}, dimensions={0}, use_global_device_ids=true | all-gather | bytes 15360 | tf_op jit(solution)/shard_map/all_gather | solution.py:204
  350.8 27.6 %all-gather.23.cloned.1.call-done = bf16[12288,192]{0,1:T(8,128)(2,1)} async-done(((bf16[768,192]{0,1:T(8,128)(2,1)}), bf16[12288,192]{0,1:T(8,128)(2,1)}) %all-gather.23.cloned.1.call-update) | async-done | bytes 4718608 | tf_op jit(solution)/shard_map/all_gather | solution.py:189
  378.3 8.3 reshape.244
  386.6 4.3 copy.112
  394.1 38.2 %all-gather.25.cloned.1.call-done = bf16[12288,192]{0,1:T(8,128)(2,1)} async-done(((bf16[768,192]{0,1:T(8,128)(2,1)}), bf16[12288,192]{0,1:T(8,128)(2,1)}) %all-gather.25.cloned.1.call-update) | async-done | bytes 4718608 | tf_op jit(solution)/shard_map/all_gather | solution.py:190
  432.2 8.3 reshape.246
  440.5 4.5 copy.113
  448.2 14.0 %all-gather.15.cloned.1.call-done = bf16[2088,768]{0,1:T(8,128)(2,1)} async-done(((bf16[2088,192]{0,1:T(8,128)(2,1)}), bf16[2088,768]{0,1:T(8,128)(2,1)}) %all-gather.15.cloned.1.call-update) | async-done | bytes 3207184 | tf_op jit(solution)/shard_map/all_gather | solution.py:24
  462.2 20.0 %multiply_convert_fusion.1 = (bf16[2088,768]{1,0:T(8,128)(2,1)S(1)}, f32[2088,768]{1,0:T(8,128)}, f32[2088,768]{1,0:T(8,128)}) fusion(f32[768]{0:T(1024)S(1)} %dynamic_slice.67, bf16[2088,768]{0,1:T(8,128)(2,1)} %all-gather.15.cloned.1.call-done, bf16[3072,768]{0,1:T(8,128)(2,1)} %bitcast.238, s32[]{:T(128)S(6)} %select_n.83), kind=kOutput, calls=%fused_computation.65 | convolution fusion | flops 2568941568 | bytes 20560900 | tf_op jit(solution)/shard_map/dot_general | solution.py:44
  483.8 6.0 convolution_convert_fusion.2
  492.0 37.2 %reduce-scatter.11.cloned.1.call-done = bf16[2088,192]{0,1:T(8,128)(2,1)} async-done(((bf16[2088,768]{0,1:T(8,128)(2,1)}), bf16[2088,192]{0,1:T(8,128)(2,1)}) %reduce-scatter.11.cloned.1.call-update) | async-done | bytes 801808 | tf_op jit(solution)/shard_map/reduce_scatter | solution.py:32
  531.4 10.6 %all-reduce.4 = (f32[2088]{0:T(1024)S(1)}, f32[2088]{0:T(1024)S(1)}) all-reduce(f32[2088]{0:T(1024)S(1)} %get-tuple-element.161, f32[2088]{0:T(1024)S(1)} %get-tuple-element.160), channel_id=1, replica_groups=mesh['dp'=2,'row'=4,'col'=4] {'col'}, use_global_device_ids=true, to_apply=%region_13.14 | all-reduce | flops 4176 | bytes 33408 | tf_op jit(solution)/shard_map/psum | solution.py:68
  543.6 3.5 reshape.248
  553.0 4.6 pad.4.clone
  563.3 10.3 all-reduce.3
  576.9 29.9 %all-gather.17.cloned.1.call-done = bf16[2088,768]{0,1:T(8,128)(2,1)} async-done(((bf16[2088,192]{0,1:T(8,128)(2,1)}), bf16[2088,768]{0,1:T(8,128)(2,1)}) %all-gather.17.cloned.1.call-update) | async-done | bytes 3207184 | tf_op jit(solution)/shard_map/all_gather | solution.py:28
  606.9 10.5 %add_convert_fusion = bf16[2088,768]{1,0:T(8,128)(2,1)S(1)} fusion(f32[2088,768]{1,0:T(8,128)} %get-tuple-element.216, f32[2088,768]{1,0:T(8,128)} %get-tuple-element.241, bf16[2088,768]{0,1:T(8,128)(2,1)} %all-gather.17.cloned.1.call-done, bf16[3072,768]{0,1:T(8,128)(2,1)} %bitcast.241, s32[]{:T(128)S(6)} %select_n.83), kind=kOutput, calls=%fused_computation.64 | convolution fusion | flops 2485555200 | bytes 20557828 | tf_op jit(solution)/shard_map/dot_general | solution.py:44
  619.0 5.9 convolution_convert_fusion.1
  625.0 39.2 %reduce-scatter.13.cloned.1.call-done = bf16[2088,192]{0,1:T(8,128)(2,1)} async-done(((bf16[2088,768]{0,1:T(8,128)(2,1)}), bf16[2088,192]{0,1:T(8,128)(2,1)}) %reduce-scatter.13.cloned.1.call-update) | async-done | bytes 801808 | tf_op jit(solution)/shard_map/reduce_scatter | solution.py:38
  664.3 5.1 multiply_reduce_fusion.3
  669.3 10.3 all-reduce.2
  682.9 30.1 %all-gather.19.cloned.1.call-done = bf16[2088,768]{0,1:T(8,128)(2,1)} async-done(((bf16[2088,192]{0,1:T(8,128)(2,1)}), bf16[2088,768]{0,1:T(8,128)(2,1)}) %all-gather.19.cloned.1.call-update) | async-done | bytes 3207184 | tf_op jit(solution)/shard_map/all_gather | solution.py:28
  713.1 3.7 convolution_convert_fusion.4
  723.6 68.2 %while.27 = (s32[]{:T(128)}, bf16[2,1044,3,64]{1,3,2,0:T(8,128)(2,1)}, bf16[2,1044,3,64]{1,3,2,0:T(8,128)(2,1)}, bf16[2,1044,3,64]{1,3,2,0:T(8,128)(2,1)}, bf16[...) while((s32[]{:T(128)}, ...), condition=%wide.region_26.27_spmd, body=%wide.region_24.26_spmd.sunk | while | flops 2124194560 | bytes 151329200 | solution.py:274
  724.5 3.4 fusion.162
  728.0 8.2 multiply_reduce_fusion.10
  736.2 8.6 multiply_convert_fusion.3
  744.8 8.3 fusion.165
  758.5 3.4 fusion.162
  762.0 8.2 multiply_reduce_fusion.10
  770.2 8.6 multiply_convert_fusion.3
  778.8 8.3 fusion.165
  799.4 5.0 fusion.72
  805.4 22.5 %all_to_all.75 = bf16[3,768,192]{2,0,1:T(4,128)(2,1)S(1)} all-to-all(bf16[3,768,192]{2,0,1:T(4,128)(2,1)S(1)} %copy.122), channel_id=1, replica_groups=mesh['dp'=2,'row'=4,'col'=4] {'col'}, dimensions={1} | all-to-all | bytes 1769472 | tf_op jit(solution)/shard_map/all_to_all | solution.py:288
  830.3 4.8 convolution_convert_fusion.5
  835.1 18.5 %all_to_all.76 = bf16[768,4,192]{0,2,1:T(8,128)(2,1)S(1)} all-to-all(bf16[768,4,192]{0,2,1:T(8,128)(2,1)S(1)} %bitcast.250), channel_id=1, replica_groups=mesh['dp'=2,'row'=4,'col'=4] {'col'}, dimensions={1} | all-to-all | bytes 2359296 | tf_op jit(solution)/shard_map/all_to_all | solution.py:297
  854.9 4.9 convolution_convert_fusion.6
  859.8 18.4 %all_to_all.77 = bf16[768,4,192]{0,2,1:T(8,128)(2,1)S(1)} all-to-all(bf16[768,4,192]{0,2,1:T(8,128)(2,1)S(1)} %bitcast.251), channel_id=1, replica_groups=mesh['dp'=2,'row'=4,'col'=4] {'col'}, dimensions={1} | all-to-all | bytes 2359296 | tf_op jit(solution)/shard_map/all_to_all | solution.py:294
  883.4 10.6 %all_to_all.78 = bf16[192,4,192]{2,0,1:T(8,128)(2,1)} all-to-all(bf16[192,4,192]{2,0,1:T(8,128)(2,1)S(1)} %copy.125), channel_id=1, replica_groups=mesh['dp'=2,'row'=4,'col'=4] {'col'}, dimensions={1} | all-to-all | bytes 589824 | tf_op jit(solution)/shard_map/all_to_all | solution.py:291
  896.1 22.9 %reduce-scatter.21.cloned.1.call-done = bf16[768,192]{0,1:T(8,128)(2,1)} async-done(((bf16[3072,192]{0,1:T(8,128)(2,1)}), bf16[768,192]{0,1:T(8,128)(2,1)}) %reduce-scatter.21.cloned.1.call-update) | async-done | bytes 294928 | tf_op jit(solution)/shard_map/reduce_scatter | solution.py:308
  919.0 21.6 %reduce-scatter.19.cloned.1.call-done = bf16[192,192]{1,0:T(8,128)(2,1)} async-done(((bf16[768,192]{1,0:T(8,128)(2,1)}), bf16[192,192]{1,0:T(8,128)(2,1)}) %reduce-scatter.19.cloned.1.call-update) | async-done | bytes 73744 | tf_op jit(solution)/shard_map/reduce_scatter | solution.py:305
  940.6 5.8 convolution_convert_fusion
  956.1 39.6 %all-reduce.1 = (f32[12,128]{1,0:T(8,128)S(1)}, f32[6,768]{1,0:T(8,128)S(1)}, f32[3072]{0:T(1024)S(1)}) all-reduce(f32[12,128]{1,0:T(8,128)S(1)} %dynamic_update_slice.26, f32[6,768]{1,0:T(8,128)S(1)} %dynamic_update_slice.27, f32[3072]{0:T(1024)S(1)} %dynamic_update_slice.28), channel_id=1, replica_groups=mesh['dp'=2,'row'=4,'col'=4] {'dp','row','col'}, use_global_device_ids=true, to_apply=%region_30.31 | all-reduce | flops 9216 | bytes 73728 | tf_op jit(solution)/shard_map/psum | solution.py:340
  1004.7 17.5 %reduce-scatter.15.cloned.1.call-done = bf16[2088,192]{0,1:T(8,128)(2,1)} async-done(((bf16[2088,768]{0,1:T(8,128)(2,1)}), bf16[2088,192]{0,1:T(8,128)(2,1)}) %reduce-scatter.15.cloned.1.call-update) | async-done | bytes 801808 | tf_op jit(solution)/shard_map/reduce_scatter | solution.py:38
  (292 shorter events, 135.5 us)
Async XLA Ops:
  7.2 173.2 %all-gather.21.cloned.1.call-start = ((), (), s32[]{:S(2)}) async-start(), calls=%async_computation.24 | async-start | bytes 1671168 | tf_op jit(solution)/shard_map/all_gather | solution.py:188
  7.9 204.8 %all-gather.13.cloned.1.call-start = ((), (), s32[]{:S(2)}) async-start(), calls=%async_computation.12 | async-start | bytes 4177920 | tf_op jit(solution)/shard_map/all_gather | solution.py:24
  13.3 309.4 %reduce-scatter.9.cloned.1.call-start = ((), (), s32[]{:S(2)}) async-start(), calls=%async_computation.13 | async-start | bytes 4177920 | tf_op jit(solution)/shard_map/reduce_scatter | solution.py:32
  13.7 1.8 collective-permute-start
  15.6 17.6 %collective-permute-start.1 = (bf16[2,3,192,192]{3,2,1,0:T(8,128)(2,1)S(1)}, bf16[2,3,192,192]{3,2,1,0:T(8,128)(2,1)S(1)}, u32[]{:S(2)}, u32[]{:S(2)}) collective-permute-start(bf16[2,3,192,192]{3,2,1,0:T(8,128)(2,1)S(1)} %maximum_select_fusion.3), channel_id=1, source_target_pairs={{0,2},{1,3},{2,0},{3,1},{4,6},{5,7},{6,4},{7,5},{8,10},{9,11},{10,... | collective-permute-start | bytes 1327112 | tf_op jit(solution)/shard_map/ppermute | solution.py:15
  18.6 53.8 %copy-start.50 = (f32[3,128]{1,0:T(4,128)S(1)}, f32[3,128]{1,0:T(4,128)}, u32[]{:S(2)}) copy-start(f32[3,128]{1,0:T(4,128)} %param.27) | copy-start | bytes 4612
  33.7 34.0 %collective-permute-start.2 = (bf16[4,3,192,192]{3,2,1,0:T(8,128)(2,1)S(1)}, bf16[4,3,192,192]{3,2,1,0:T(8,128)(2,1)}, u32[]{:S(2)}, u32[]{:S(2)}) collective-permute-start(bf16[4,3,192,192]{3,2,1,0:T(8,128)(2,1)S(1)} %maximum_select_fusion.2), channel_id=1, source_target_pairs={{0,4},{1,5},{2,6},{3,7},{4,0},{5,1},{6,2},{7,3},{8,12},{9,13},{10,... | collective-permute-start | bytes 2654216 | tf_op jit(solution)/shard_map/ppermute | solution.py:15
  69.8 118.3 %collective-permute-start.3 = (bf16[8,3,192,192]{3,2,1,0:T(8,128)(2,1)S(1)}, bf16[8,3,192,192]{3,2,1,0:T(8,128)(2,1)}, u32[]{:S(2)}, u32[]{:S(2)}) collective-permute-start(bf16[8,3,192,192]{3,2,1,0:T(8,128)(2,1)S(1)} %maximum_select_fusion.1), channel_id=1, source_target_pairs={{0,8},{1,9},{2,10},{3,11},{4,12},{5,13},{6,14},{7,15},{8,0},{9,1},... | collective-permute-start | bytes 5308424 | tf_op jit(solution)/shard_map/ppermute | solution.py:15
  242.1 7.8 copy-start.30
  242.1 8.4 copy-start.34
  267.6 7.8 copy-start.30
  267.6 8.4 copy-start.34
  276.1 5.1 copy-start.3
  276.1 9.1 copy-start.5
  285.2 37.5 %copy-start.1 = (bf16[2088,192]{0,1:T(8,128)(2,1)S(1)}, bf16[2088,192]{0,1:T(8,128)(2,1)}, u32[]{:S(2)}) copy-start(bf16[2088,192]{0,1:T(8,128)(2,1)} %reshape.238) | copy-start | bytes 2405380
  285.2 37.5 %copy-start.39 = (f32[192]{0:T(256)S(1)}, f32[192]{0:T(256)}, u32[]{:S(2)}) copy-start(f32[192]{0:T(256)} %param.29) | copy-start | bytes 2308
  285.2 49.5 %copy-start.42 = (f32[192]{0:T(256)S(1)}, f32[192]{0:T(256)}, u32[]{:S(2)}) copy-start(f32[192]{0:T(256)} %param.30) | copy-start | bytes 2308
  285.2 49.5 %copy-start.44 = (f32[192]{0:T(256)S(1)}, f32[192]{0:T(256)}, u32[]{:S(2)}) copy-start(f32[192]{0:T(256)} %param.31) | copy-start | bytes 2308
  285.3 52.1 %copy-start.48 = (f32[768]{0:T(1024)S(1)}, f32[768]{0:T(1024)}, u32[]{:S(2)}) copy-start(f32[768]{0:T(1024)} %param.33) | copy-start | bytes 9220
  285.3 93.1 %all-gather.23.cloned.1.call-start = ((), (), s32[]{:S(2)}) async-start(), calls=%async_computation.25 | async-start | bytes 5013504 | tf_op jit(solution)/shard_map/all_gather | solution.py:189
  285.9 146.4 %all-gather.25.cloned.1.call-start = ((), (), s32[]{:S(2)}) async-start(), calls=%async_computation.26 | async-start | bytes 5013504 | tf_op jit(solution)/shard_map/all_gather | solution.py:190
  286.4 175.8 %all-gather.15.cloned.1.call-start = ((), (), s32[]{:S(2)}) async-start(), calls=%async_computation.14 | async-start | bytes 4177920 | tf_op jit(solution)/shard_map/all_gather | solution.py:24
  334.6 344.9 %copy-start.25 = (f32[2088]{0:T(1024)}, f32[2088]{0:T(1024)S(1)}, u32[]{:S(2)}) copy-start(f32[2088]{0:T(1024)S(1)} %get-tuple-element.235) | copy-start | bytes 25060
  334.7 344.9 %copy-start.27 = (f32[2088]{0:T(1024)}, f32[2088]{0:T(1024)S(1)}, u32[]{:S(2)}) copy-start(f32[2088]{0:T(1024)S(1)} %get-tuple-element.236) | copy-start | bytes 25060
  337.4 191.8 %reduce-scatter.11.cloned.1.call-start = ((), (), s32[]{:S(2)}) async-start(), calls=%async_computation.15 | async-start | bytes 4177920 | tf_op jit(solution)/shard_map/reduce_scatter | solution.py:32
  489.8 39.3 %copy-start.8 = (bf16[2088,192]{0,1:T(8,128)(2,1)S(1)}, bf16[2088,192]{0,1:T(8,128)(2,1)}, u32[]{:S(2)}) copy-start(bf16[2088,192]{0,1:T(8,128)(2,1)} %reduce-scatter.9.cloned.1.call-done) | copy-start | bytes 2405380
  489.8 39.3 %copy-start.51 = (f32[192]{0:T(256)S(1)}, f32[192]{0:T(256)}, u32[]{:S(2)}) copy-start(f32[192]{0:T(256)} %param.35) | copy-start | bytes 2308
  489.8 52.2 %copy-start.41 = (f32[192]{0:T(256)S(1)}, f32[192]{0:T(256)}, u32[]{:S(2)}) copy-start(f32[192]{0:T(256)} %param.36) | copy-start | bytes 2308
  489.8 52.2 %copy-start.52 = (f32[192]{0:T(256)S(1)}, f32[192]{0:T(256)}, u32[]{:S(2)}) copy-start(f32[192]{0:T(256)} %param.37) | copy-start | bytes 2308
  489.9 117.0 %all-gather.17.cloned.1.call-start = ((), (), s32[]{:S(2)}) async-start(), calls=%async_computation.16 | async-start | bytes 4177920 | tf_op jit(solution)/shard_map/all_gather | solution.py:28
  576.4 87.8 %reduce-scatter.13.cloned.1.call-start = ((), (), s32[]{:S(2)}) async-start(), calls=%async_computation.17 | async-start | bytes 4177920 | tf_op jit(solution)/shard_map/reduce_scatter | solution.py:38
  625.0 88.1 %all-gather.19.cloned.1.call-start = ((), (), s32[]{:S(2)}) async-start(), calls=%async_computation.18 | async-start | bytes 4177920 | tf_op jit(solution)/shard_map/all_gather | solution.py:28
  679.6 37.2 %copy-start.35 = (f32[2088]{0:T(1024)}, f32[2088]{0:T(1024)S(1)}, u32[]{:S(2)}) copy-start(f32[2088]{0:T(1024)S(1)} %broadcast_multiply_fusion) | copy-start | bytes 25060
  679.6 37.2 %copy-start.37 = (f32[2088]{0:T(1024)}, f32[2088]{0:T(1024)S(1)}, u32[]{:S(2)}) copy-start(f32[2088]{0:T(1024)S(1)} %broadcast_multiply_fusion.1) | copy-start | bytes 25060
  682.7 211.4 %reduce-scatter.17.cloned.1.call-start = ((), (), s32[]{:S(2)}) async-start(), calls=%async_computation.20 | async-start | bytes 1474560 | tf_op jit(solution)/shard_map/reduce_scatter | solution.py:302
  716.8 6.9 copy-start.4
  716.8 6.9 copy-start.6
  716.8 6.9 copy-start.32
  736.2 8.6 copy-start.7
  744.8 8.3 copy-start
  744.8 8.3 copy-start.17
  770.2 8.6 copy-start.7
  778.8 8.3 copy-start
  778.8 8.3 copy-start.17
  829.1 67.0 %reduce-scatter.23.cloned.1.call-start = ((), (), s32[]{:S(2)}) async-start(), calls=%async_computation.23 | async-start | bytes 1474560 | tf_op jit(solution)/shard_map/reduce_scatter | solution.py:311
  835.1 19.8 %copy-start.22 = (bf16[2088,768]{1,0:T(8,128)(2,1)S(1)}, bf16[2088,768]{1,0:T(8,128)(2,1)}, u32[]{:S(2)}) copy-start(bf16[2088,768]{1,0:T(8,128)(2,1)} %copy-done.21) | copy-start | bytes 9621508
  854.8 64.2 %reduce-scatter.21.cloned.1.call-start = ((), (), s32[]{:S(2)}) async-start(), calls=%async_computation.22 | async-start | bytes 1474560 | tf_op jit(solution)/shard_map/reduce_scatter | solution.py:308
  859.8 20.1 %copy-start.13 = (bf16[2088,192]{0,1:T(8,128)(2,1)S(1)}, bf16[2088,192]{0,1:T(8,128)(2,1)}, u32[]{:S(2)}) copy-start(bf16[2088,192]{0,1:T(8,128)(2,1)} %copy-done.12) | copy-start | bytes 2405380
  879.4 61.2 %reduce-scatter.19.cloned.1.call-start = ((), (), s32[]{:S(2)}) async-start(), calls=%async_computation.21 | async-start | bytes 491520 | tf_op jit(solution)/shard_map/reduce_scatter | solution.py:305
  883.0 57.7 %copy-start.15 = (bf16[2088,576]{0,1:T(8,128)(2,1)S(1)}, bf16[2088,576]{0,1:T(8,128)(2,1)}, u32[]{:S(2)}) copy-start(bf16[2088,576]{0,1:T(8,128)(2,1)} %reshape.251) | copy-start | bytes 7216132
  894.0 103.6 %all-reduce.9.cloned.1.call-start = ((), (), s32[]{:S(2)}) async-start(), calls=%async_computation.27 | async-start | bytes 1966080 | tf_op jit(solution)/shard_map/psum | solution.py:316
  940.6 81.6 %reduce-scatter.15.cloned.1.call-start = ((), (), s32[]{:S(2)}) async-start(), calls=%async_computation.19 | async-start | bytes 4177920 | tf_op jit(solution)/shard_map/reduce_scatter | solution.py:38
  948.2 4.8 copy-start.46
  948.2 4.9 copy-start.47
  948.2 4.9 copy-start.49
  951.3 70.9 %copy-start.2 = (bf16[2088,192]{0,1:T(8,128)(2,1)S(1)}, bf16[2088,192]{0,1:T(8,128)(2,1)}, u32[]{:S(2)}) copy-start(bf16[2088,192]{0,1:T(8,128)(2,1)} %reshape.238) | copy-start | bytes 2405380
  951.3 70.9 %copy-start.9 = (bf16[2088,192]{0,1:T(8,128)(2,1)S(1)}, bf16[2088,192]{0,1:T(8,128)(2,1)}, u32[]{:S(2)}) copy-start(bf16[2088,192]{0,1:T(8,128)(2,1)} %reduce-scatter.9.cloned.1.call-done) | copy-start | bytes 2405380
  951.3 70.9 %copy-start.11 = (f32[2088,192]{0,1:T(8,128)S(1)}, f32[2088,192]{0,1:T(8,128)}, u32[]{:S(2)}) copy-start(f32[2088,192]{0,1:T(8,128)} %get-tuple-element.213) | copy-start | bytes 4810756
  951.3 70.9 %copy-start.26 = (f32[2088]{0:T(1024)S(1)}, f32[2088]{0:T(1024)}, u32[]{:S(2)}) copy-start(f32[2088]{0:T(1024)} %copy-done.25) | copy-start | bytes 25060
  951.3 70.9 %copy-start.28 = (f32[2088]{0:T(1024)S(1)}, f32[2088]{0:T(1024)}, u32[]{:S(2)}) copy-start(f32[2088]{0:T(1024)} %copy-done.27) | copy-start | bytes 25060
  951.4 70.9 %copy-start.36 = (f32[2088]{0:T(1024)S(1)}, f32[2088]{0:T(1024)}, u32[]{:S(2)}) copy-start(f32[2088]{0:T(1024)} %copy-done.35) | copy-start | bytes 25060
  951.4 70.9 %copy-start.38 = (f32[2088]{0:T(1024)S(1)}, f32[2088]{0:T(1024)}, u32[]{:S(2)}) copy-start(f32[2088]{0:T(1024)} %copy-done.37) | copy-start | bytes 25060
  951.4 70.9 %copy-start.40 = (f32[192]{0:T(256)S(1)}, f32[192]{0:T(256)}, u32[]{:S(2)}) copy-start(f32[192]{0:T(256)} %param.29) | copy-start | bytes 2308
  951.4 70.9 %copy-start.43 = (f32[192]{0:T(256)S(1)}, f32[192]{0:T(256)}, u32[]{:S(2)}) copy-start(f32[192]{0:T(256)} %param.30) | copy-start | bytes 2308
  (21 other events, 40.2 us)
Sparse Core Ops, SparseCore 0:
  10.3 44.6 all-gather.20
  56.5 29.2 all-gather.12
  285.4 37.2 reduce-scatter.8
  324.8 53.5 all-gather.22
  380.4 51.7 all-gather.24
  434.2 27.9 all-gather.14
  490.0 39.1 reduce-scatter.10
  576.6 30.2 all-gather.16
  625.1 39.1 reduce-scatter.12
  682.8 30.1 all-gather.18
  829.2 29.3 reduce-scatter.16
  860.8 27.9 reduce-scatter.22
  891.0 27.9 reduce-scatter.20
  921.1 19.3 reduce-scatter.18
  943.5 37.1 all-reduce.8
  983.1 39.0 reduce-scatter.14
